TPU v7x, 32 devices: a whole 2x2x4 slice. The times are simulated.
32 devices in a mesh: dp: 2 (over x), space: 16 (over z, y, core).
Axes of the slice: x: 2, y: 2, z: 4, core: 2. Of those that a mesh axis runs over, the one named last changes fastest.
Arguments:
- stash: bfloat16 [16, 16, 4, 8640], P('space', None, 'dp'), may hold values from -5 to 5
- piece_map: int32 [16, 16], P(None, 'space'), may hold values from 0 to 15, as said below
- gain_one: float32 [768], replicated, may hold values from 0.5 to 1.5
- spec_one: float32 [2, 8, 96, 96], replicated, may hold values from -0.4375 to 0.4375
- bias_one: float32 [2, 768], replicated, may hold values from -3 to 3
- spec_two: float32 [2, 8, 96, 96], replicated, may hold values from -0.4375 to 0.4375
- bias_two: float32 [2, 768], replicated, may hold values from -0.6 to 0.6
- gain_two: float32 [768], replicated, may hold values from 0.5 to 1.5
- fc_one: bfloat16 [768, 3072], replicated, may hold values from -0.21875 to 0.21875
- bias_fc: float32 [3072], replicated, may hold values from -3 to 3
- fc_two: bfloat16 [3072, 768], replicated, may hold values from -0.109375 to 0.109375
- cotangent: bfloat16 [4, 16, 180, 768], P('dp', 'space'), may hold values from -6 to 6
Outputs:
- grad_input: float32 [4, 16, 180, 768], P('dp', 'space')
- grad_fc_one: float32 [768, 3072], P(None, ('dp', 'space'))
- grad_fc_two: float32 [3072, 768], P(('dp', 'space'))
- grad_bias_fc: float32 [3072], replicated
- grad_bias_out: float32 [768], replicated
- grad_gain_one: float32 [768], replicated
- grad_gain_two: float32 [768], replicated
- grad_spec_one: float32 [2, 8, 96, 96], replicated
- grad_bias_one: float32 [2, 768], replicated
- grad_spec_two: float32 [2, 8, 96, 96], replicated
- grad_bias_two: float32 [2, 768], replicated
Inputs may be any that keep to these rules, and one draw needn't show every extreme that they name: `piece_map`: each column holds every number from 0 to 15 once.
All inputs are finite; a program needn't handle non-finite values.
Results may differ from a plain program's by a relative error of at most 0.0046.
Values may be sent and summed in bfloat16 or wider, within the bound.
A program may use at most 128 MiB of HBM per device.

v0:
```python
import math
import jax
import jax.numpy as jnp
from jax import lax
from jax.sharding import PartitionSpec as P

KW = 64
epsilon = 1e-05
highest = lax.Precision.HIGHEST


def layer_norm(values, gain_vector):
    centred = values - jnp.mean(values, axis=-1, keepdims=True)
    spread = jnp.mean(centred * centred, axis=-1, keepdims=True)
    return centred * lax.rsqrt(spread + epsilon) * gain_vector


def smooth_gate(values):
    return jax.nn.gelu(values, approximate=True)


def block_mix(real_part, imag_part, weights, biases):
    blocks = weights.shape[1]
    width_block = weights.shape[2]
    leading = real_part.shape[:-1]
    real_blocks = real_part.reshape(leading + (blocks, width_block))
    imag_blocks = imag_part.reshape(leading + (blocks, width_block))
    bias_real = biases[0].reshape(blocks, width_block)
    bias_imag = biases[1].reshape(blocks, width_block)
    new_real = (
        jnp.einsum("...ni,nio->...no", real_blocks, weights[0], precision=highest)
        - jnp.einsum("...ni,nio->...no", imag_blocks, weights[1], precision=highest)
        + bias_real
    )
    new_imag = (
        jnp.einsum("...ni,nio->...no", real_blocks, weights[1], precision=highest)
        + jnp.einsum("...ni,nio->...no", imag_blocks, weights[0], precision=highest)
        + bias_imag
    )
    return (
        new_real.reshape(leading + (blocks * width_block,)),
        new_imag.reshape(leading + (blocks * width_block,)),
    )


def spectral_mlp(spec_real, spec_imag, spec_one, bias_one, spec_two, bias_two):
    inner_real, inner_imag = block_mix(spec_real, spec_imag, spec_one, bias_one)
    return block_mix(smooth_gate(inner_real), smooth_gate(inner_imag), spec_two, bias_two)


def wave_tables(length, total_modes):
    positions = jnp.arange(length, dtype=jnp.int32)
    frequency = jnp.arange(total_modes, dtype=jnp.int32)
    phases = positions[:, None] * frequency[None, :] % length
    angles = phases.astype(jnp.float32) * (2.0 * math.pi / length)
    factor = 1.0 / math.sqrt(length)
    return (jnp.cos(angles) * factor, jnp.sin(angles) * factor)


def meridian_apply(table, field):
    return jnp.einsum("hk,bhmd->bkmd", table, field, precision=highest)


def meridian_forward(real_part, imag_part, merid_cos, merid_sin):
    new_real = meridian_apply(merid_cos, real_part) + meridian_apply(merid_sin, imag_part)
    new_imag = meridian_apply(merid_cos, imag_part) - meridian_apply(merid_sin, real_part)
    return (new_real, new_imag)


def meridian_inverse(real_part, imag_part, merid_cos, merid_sin):
    new_real = meridian_apply(merid_cos, real_part) - meridian_apply(merid_sin, imag_part)
    new_imag = meridian_apply(merid_cos, imag_part) + meridian_apply(merid_sin, real_part)
    return (new_real, new_imag)


def zonal_project(field, table):
    return jnp.einsum("brwd,wk->brkd", field, table, precision=highest)


def zonal_expand(field, table):
    return jnp.einsum("brkd,wk->brwd", field, table, precision=highest)


def local(
    stash,
    piece_map,
    gain_one,
    spec_one,
    bias_one,
    spec_two,
    bias_two,
    gain_two,
    fc_one,
    bias_fc,
    fc_two,
    cotangent,
):
    samples, lat_rows, lon_cells, model_width = cotangent.shape
    space_ranks = lax.axis_size("space")
    lat_total = lat_rows * space_ranks
    tokens = samples * lat_rows * lon_cells
    arrived = lax.all_to_all(stash, "space", split_axis=1, concat_axis=0, tiled=True)
    ordering = jnp.argsort(piece_map[:, 0])
    placed = jnp.take(arrived[:, 0], ordering, axis=0)
    inputs = jnp.transpose(placed, (1, 0, 2)).reshape(samples, lat_rows, lon_cells, model_width)
    base_field = inputs.astype(jnp.float32)
    zonal_cos, zonal_sin = wave_tables(lon_cells, KW)
    doubling = jnp.where(jnp.arange(KW) == 0, 1.0, 2.0).astype(jnp.float32)
    back_cos = zonal_cos * doubling
    back_sin = zonal_sin * doubling
    merid_cos, merid_sin = wave_tables(lat_total, lat_total)
    normed, pull_one = jax.vjp(layer_norm, base_field, gain_one)
    zonal_real = zonal_project(normed, zonal_cos)
    zonal_imag = -zonal_project(normed, zonal_sin)
    modes_real, modes_imag = (
        lax.all_to_all(zonal_real, "space", split_axis=2, concat_axis=1, tiled=True),
        lax.all_to_all(zonal_imag, "space", split_axis=2, concat_axis=1, tiled=True),
    )
    spec_real, spec_imag = meridian_forward(modes_real, modes_imag, merid_cos, merid_sin)
    mixed_spec, pull_mix = jax.vjp(
        spectral_mlp, spec_real, spec_imag, spec_one, bias_one, spec_two, bias_two
    )
    back_real, back_imag = meridian_inverse(mixed_spec[0], mixed_spec[1], merid_cos, merid_sin)
    rows_real, rows_imag = (
        lax.all_to_all(back_real, "space", split_axis=1, concat_axis=2, tiled=True),
        lax.all_to_all(back_imag, "space", split_axis=1, concat_axis=2, tiled=True),
    )
    spatial = zonal_expand(rows_real, back_cos) - zonal_expand(rows_imag, back_sin)
    mixed_field = base_field + normed + spatial
    normed_two, pull_two = jax.vjp(layer_norm, mixed_field, gain_two)
    normed_flat = normed_two.astype(jnp.bfloat16).reshape(tokens, model_width)
    hidden_pre = jnp.dot(normed_flat, fc_one, preferred_element_type=jnp.float32) + bias_fc
    active, pull_gate = jax.vjp(smooth_gate, hidden_pre)
    active_flat = active.astype(jnp.bfloat16)
    upstream = cotangent.reshape(tokens, model_width)
    grad_active = jnp.einsum("td,fd->tf", upstream, fc_two, preferred_element_type=jnp.float32)
    grad_hidden = pull_gate(grad_active)[0]
    grad_hidden_flat = grad_hidden.astype(jnp.bfloat16)
    grad_normed_two = jnp.einsum(
        "tf,df->td", grad_hidden_flat, fc_one, preferred_element_type=jnp.float32
    )
    term_one = jnp.einsum(
        "td,tf->df", normed_flat, grad_hidden_flat, preferred_element_type=jnp.float32
    )
    term_two = jnp.einsum("td,tf->df", upstream, active_flat, preferred_element_type=jnp.float32)
    grad_mixed_norm, grad_gain_two = pull_two(grad_normed_two.reshape(mixed_field.shape))
    grad_mixed = cotangent.astype(jnp.float32) + grad_mixed_norm
    grad_back_real = zonal_project(grad_mixed, back_cos)
    grad_back_imag = -zonal_project(grad_mixed, back_sin)
    grad_modes_real, grad_modes_imag = (
        lax.all_to_all(grad_back_real, "space", split_axis=2, concat_axis=1, tiled=True),
        lax.all_to_all(grad_back_imag, "space", split_axis=2, concat_axis=1, tiled=True),
    )
    grad_out_real, grad_out_imag = meridian_forward(
        grad_modes_real, grad_modes_imag, merid_cos, merid_sin
    )
    pulled = pull_mix((grad_out_real, grad_out_imag))
    grad_merid_real, grad_merid_imag = meridian_inverse(pulled[0], pulled[1], merid_cos, merid_sin)
    grad_rows_real, grad_rows_imag = (
        lax.all_to_all(grad_merid_real, "space", split_axis=1, concat_axis=2, tiled=True),
        lax.all_to_all(grad_merid_imag, "space", split_axis=1, concat_axis=2, tiled=True),
    )
    grad_normed = (
        grad_mixed
        + zonal_expand(grad_rows_real, zonal_cos)
        - zonal_expand(grad_rows_imag, zonal_sin)
    )
    grad_base, grad_gain_one = pull_one(grad_normed)
    grad_input = grad_mixed + grad_base
    bias_sum = jnp.sum(grad_hidden, axis=0)
    out_sum = jnp.sum(cotangent, axis=(0, 1, 2), dtype=jnp.float32)
    totals = lax.psum(
        (
            grad_gain_one,
            grad_gain_two,
            pulled[2],
            pulled[3],
            pulled[4],
            pulled[5],
            bias_sum,
            out_sum,
        ),
        ("dp", "space"),
    )
    paired = (
        lax.psum_scatter(term_one, "dp", scatter_dimension=1, tiled=True),
        lax.psum_scatter(term_two, "dp", scatter_dimension=1, tiled=True),
    )
    summed = (
        lax.psum_scatter(paired[0], "space", scatter_dimension=1, tiled=True),
        lax.psum_scatter(paired[1], "space", scatter_dimension=1, tiled=True),
    )
    grad_scale = 1.0 / math.sqrt(samples * lax.axis_size("dp") * lat_total * lon_cells)
    return (
        grad_input,
        summed[0] * grad_scale,
        (summed[1] * grad_scale).T,
        totals[6] * grad_scale,
        totals[7] * grad_scale,
        totals[0] * grad_scale,
        totals[1] * grad_scale,
        totals[2] * grad_scale,
        totals[3] * grad_scale,
        totals[4] * grad_scale,
        totals[5] * grad_scale,
    )


def solution(mesh):
    placed = (
        P("space", None, "dp", None),
        P(None, "space"),
        P(),
        P(),
        P(),
        P(),
        P(),
        P(),
        P(),
        P(),
        P(),
        P("dp", "space", None, None),
    )
    return jax.shard_map(
        local,
        mesh=mesh,
        in_specs=placed,
        out_specs=(
            P("dp", "space", None, None),
            P(None, ("dp", "space")),
            P(("dp", "space"), None),
            P(),
            P(),
            P(),
            P(),
            P(),
            P(),
            P(),
            P(),
        ),
        check_vma=False,
    )
```

profile of v0, /device:TPU:0, one launch (start us, length us, event | category | flops | bytes accessed | tf_op | source)
XLA Modules:
  0.0 540.8 jit_solution(15111530025571040540)
XLA Ops:
  8.0 7.4 %all-to-all-start = ((bf16[1,16,2,8640]{3,2,0,1:T(2,128)(2,1)}), bf16[1,16,2,8640]{3,2,0,1:T(2,128)(2,1)S(1)}, u32[]{:S(2)}, u32[]{:S(2)}) async-start(bf16[1,16,2,8640]{3,2,0,1:T(2,128)(2,1)} %bitcast.441), calls=%async_computation | async-start | bytes 1114112 | tf_op jit(solution)/shard_map/all_to_all | solution.py:102
  17.4 12.9 %all-to-all-done = bf16[1,16,2,8640]{3,2,0,1:T(2,128)(2,1)S(1)} async-done(((bf16[1,16,2,8640]{3,2,0,1:T(2,128)(2,1)}), bf16[1,16,2,8640]{3,2,0,1:T(2,128)(2,1)S(1)}, u32[]{:S(2)}, u32[]{:S(2)}) %all-to-all-start) | async-done | bytes 552992 | tf_op jit(solution)/shard_map/all_to_all | solution.py:102
  37.2 4.3 all-to-all-start.1
  43.9 9.8 %all-to-all-done.1 = f32[2,1,64,768]{3,0,1,2:T(2,128)S(1)} async-done(((f32[2,1,64,768]{3,0,1,2:T(2,128)}), f32[2,1,64,768]{3,0,1,2:T(2,128)S(1)}, u32[]{:S(2)}, u32[]{:S(2)}) %all-to-all-start.1) | async-done | bytes 393248 | tf_op jit(solution)/shard_map/all_to_all | solution.py:116
  53.7 4.0 all-to-all-start.2
  59.5 10.4 %all-to-all-done.2 = f32[2,1,64,768]{3,0,1,2:T(2,128)S(1)} async-done(((f32[2,1,64,768]{3,0,1,2:T(2,128)}), f32[2,1,64,768]{3,0,1,2:T(2,128)S(1)}, u32[]{:S(2)}, u32[]{:S(2)}) %all-to-all-start.2) | async-done | bytes 393248 | tf_op jit(solution)/shard_map/all_to_all | solution.py:117
  95.5 9.1 %all-to-all-done.3 = f32[2,16,4,768]{3,2,0,1:T(4,128)S(1)} async-done(((f32[2,16,4,768]{3,2,0,1:T(4,128)}), f32[2,16,4,768]{3,2,0,1:T(4,128)S(1)}, u32[]{:S(2)}, u32[]{:S(2)}) %all-to-all-start.3) | async-done | bytes 393248 | tf_op jit(solution)/shard_map/all_to_all | solution.py:125
  108.2 6.3 %fusion.368 = f32[360,3072]{1,0:T(8,128)} fusion(bf16[360,768]{1,0:T(8,128)(2,1)S(1)} %copy-done.24, bf16[3072,768]{1,0:T(8,128)(2,1)} %param.22), kind=kOutput, calls=%fused_computation.459 | convolution fusion | flops 1698693120 | bytes 9695232 | tf_op jit(solution)/shard_map/td,fd->tf/dot_general | solution.py:136
  116.1 4.2 all-to-all-done.4
  123.4 9.3 %fusion.363 = (f32[3072]{0:T(1024)S(1)}, bf16[360,3072]{1,0:T(8,128)(2,1)S(1)}, f32[360,3072]{1,0:T(8,128)}) fusion(f32[360,3072]{1,0:T(8,128)} %fusion.368, f32[3072]{0:T(1024)S(1)} %copy-done.30, bf16[360,768]{1,0:T(8,128)(2,1)S(1)} %reshape.380, bf16[768,3072]{1,0:T(8,128)(2,1)} %param.20), kind=kOutput, calls=%fused_computation.455 | convolution fusion | flops 1723020288 | bytes 16355328 | tf_op jit(solution)/shard_map/dot_general | solution.py:132
  134.2 5.1 fusion.32
  140.4 8.9 %convolution_bitcast_fusion = f32[768,3072]{0,1:T(8,128)} fusion(bf16[360,768]{1,0:T(8,128)(2,1)S(1)} %copy-done.25, f32[360,3072]{1,0:T(8,128)} %get-tuple-element.83), kind=kOutput, calls=%fused_computation.3 | convolution fusion | flops 1708646400 | bytes 14413824 | tf_op jit(solution)/shard_map/td,tf->df/dot_general | solution.py:145
  149.3 6.0 %fusion.34 = f32[360,768]{1,0:T(8,128)} fusion(bf16[768,3072]{1,0:T(8,128)(2,1)} %param.20, bf16[360,3072]{1,0:T(8,128)(2,1)} %copy-done.17), kind=kOutput, calls=%fused_computation.86 | convolution fusion | flops 1698693120 | bytes 8036352 | tf_op jit(solution)/shard_map/tf,df->td/dot_general | solution.py:139
  168.4 10.0 %all-to-all-done.6 = f32[2,1,64,768]{3,0,1,2:T(2,128)S(1)} async-done(((f32[2,1,64,768]{3,0,1,2:T(2,128)}), f32[2,1,64,768]{3,0,1,2:T(2,128)S(1)}, u32[]{:S(2)}, u32[]{:S(2)}) %all-to-all-start.6) | async-done | bytes 393248 | tf_op jit(solution)/shard_map/all_to_all | solution.py:151
  183.7 10.3 %all-to-all-done.5 = f32[2,1,64,768]{3,0,1,2:T(2,128)S(1)} async-done(((f32[2,1,64,768]{3,0,1,2:T(2,128)}), f32[2,1,64,768]{3,0,1,2:T(2,128)S(1)}, u32[]{:S(2)}, u32[]{:S(2)}) %all-to-all-start.5) | async-done | bytes 393248 | tf_op jit(solution)/shard_map/all_to_all | solution.py:152
  216.7 33.6 %reduce-scatter.9.cloned.1.call-done = f32[768,1536]{1,0:T(8,128)} async-done(((f32[768,3072]{1,0:T(8,128)}), f32[768,1536]{1,0:T(8,128)}) %reduce-scatter.9.cloned.1.call-update) | async-done | bytes 4718608 | tf_op jit(solution)/shard_map/reduce_scatter | solution.py:186
  250.3 6.1 %copy.208 = f32[768,1536]{0,1:T(8,128)} copy(f32[768,1536]{1,0:T(8,128)} %reduce-scatter.9.cloned.1.call-done) | data formatting | bytes 9437184
  256.5 108.2 %reduce-scatter.11.cloned.1.call-done = f32[768,1536]{0,1:T(8,128)} async-done(((f32[768,3072]{0,1:T(8,128)}), f32[768,1536]{0,1:T(8,128)}) %reduce-scatter.11.cloned.1.call-update) | async-done | bytes 4718608 | tf_op jit(solution)/shard_map/reduce_scatter | solution.py:187
  378.2 5.6 %all-to-all-start.8 = ((f32[2,16,4,768]{3,2,0,1:T(4,128)}), f32[2,16,4,768]{3,2,0,1:T(4,128)S(1)}, u32[]{:S(2)}, u32[]{:S(2)}) async-start(f32[2,16,4,768]{3,2,0,1:T(4,128)} %copy.176), calls=%async_computation.8 | async-start | bytes 786432 | tf_op jit(solution)/shard_map/all_to_all | solution.py:161
  385.9 10.2 %all-to-all-done.8 = f32[2,16,4,768]{3,2,0,1:T(4,128)S(1)} async-done(((f32[2,16,4,768]{3,2,0,1:T(4,128)}), f32[2,16,4,768]{3,2,0,1:T(4,128)S(1)}, u32[]{:S(2)}, u32[]{:S(2)}) %all-to-all-start.8) | async-done | bytes 393248 | tf_op jit(solution)/shard_map/all_to_all | solution.py:161
  396.2 4.0 all-to-all-start.7
  400.4 43.3 %all-reduce.16.cloned.1.call-done = (f32[2,8,96,96]{3,2,1,0:T(8,128)}, f32[2,8,96,96]{3,2,1,0:T(8,128)}) async-done(((f32[2,8,96,96]{3,2,1,0:T(8,128)}, f32[2,8,96,96]{3,2,1,0:T(8,128)}), (f32[2,8,96,96]{3,2,1,0:T(8,128)}, f32[2,8,96,96]{3,2,1,0:T(8,128)})) %all-reduce.16.cloned.1.call-update) | async-done | bytes 1179664 | tf_op jit(solution)/shard_map/psum | solution.py:172
  453.0 41.9 %all-reduce.12 = (f32[3072]{0:T(1024)S(1)}, f32[768]{0:T(1024)S(1)}, f32[768]{0:T(1024)S(1)}, f32[768]{0:T(1024)S(1)}, f32[2,768]{1,0:T(2,128)S(1)}, /*index=5*/f32[2,768]{1,0:T(2,128)S(1)}) all-reduce(f32[3072]{0:T(1024)S(1)} %get-tuple-element.73, ...), channel_id=1, replica_groups=mesh['dp'=2,'space'=16] {'dp','space'}, use_global_device_ids=true, to_apply=%region_14.15 | all-reduce | flops 8448 | bytes 67584 | tf_op jit(solution)/shard_map/psum | solution.py:172
  499.4 32.0 %reduce-scatter.15.cloned.1.call-done = f32[96,768]{1,0:T(8,128)} async-done(((f32[1536,768]{1,0:T(8,128)}), f32[96,768]{1,0:T(8,128)}) %reduce-scatter.15.cloned.1.call-update) | async-done | bytes 294928
  (210 shorter events, 121.3 us)
Async XLA Ops:
  8.0 22.2 %all-to-all-start = ((bf16[1,16,2,8640]{3,2,0,1:T(2,128)(2,1)}), bf16[1,16,2,8640]{3,2,0,1:T(2,128)(2,1)S(1)}, u32[]{:S(2)}, u32[]{:S(2)}) async-start(bf16[1,16,2,8640]{3,2,0,1:T(2,128)(2,1)} %bitcast.441), calls=%async_computation | async-start | bytes 1114112 | tf_op jit(solution)/shard_map/all_to_all | solution.py:102
  37.2 16.5 %all-to-all-start.1 = ((f32[2,1,64,768]{3,0,1,2:T(2,128)}), f32[2,1,64,768]{3,0,1,2:T(2,128)S(1)}, u32[]{:S(2)}, u32[]{:S(2)}) async-start(f32[2,1,64,768]{3,0,1,2:T(2,128)} %copy.140), calls=%async_computation.1 | async-start | bytes 786432 | tf_op jit(solution)/shard_map/all_to_all | solution.py:116
  42.8 14.9 %copy-start.28 = (f32[2,768]{1,0:T(2,128)S(1)}, f32[2,768]{1,0:T(2,128)}, u32[]{:S(2)}) copy-start(f32[2,768]{1,0:T(2,128)} %param.16) | copy-start | bytes 18436
  42.8 15.1 %copy-start.29 = (f32[2,768]{1,0:T(2,128)S(1)}, f32[2,768]{1,0:T(2,128)}, u32[]{:S(2)}) copy-start(f32[2,768]{1,0:T(2,128)} %param.18) | copy-start | bytes 18436
  53.7 16.1 %all-to-all-start.2 = ((f32[2,1,64,768]{3,0,1,2:T(2,128)}), f32[2,1,64,768]{3,0,1,2:T(2,128)S(1)}, u32[]{:S(2)}, u32[]{:S(2)}) async-start(f32[2,1,64,768]{3,0,1,2:T(2,128)} %copy.142), calls=%async_computation.2 | async-start | bytes 786432 | tf_op jit(solution)/shard_map/all_to_all | solution.py:117
  73.2 2.1 copy-start.1
  73.2 2.1 copy-start.23
  78.0 3.7 copy-start.3
  79.3 2.4 copy-start.20
  87.1 5.3 copy-start.18
  88.7 15.8 %all-to-all-start.3 = ((f32[2,16,4,768]{3,2,0,1:T(4,128)}), f32[2,16,4,768]{3,2,0,1:T(4,128)S(1)}, u32[]{:S(2)}, u32[]{:S(2)}) async-start(f32[2,16,4,768]{3,2,0,1:T(4,128)} %copy.152), calls=%async_computation.3 | async-start | bytes 786432 | tf_op jit(solution)/shard_map/all_to_all | solution.py:125
  94.4 13.7 %copy-start.24 = (bf16[360,768]{1,0:T(8,128)(2,1)S(1)}, bf16[360,768]{1,0:T(8,128)(2,1)}, u32[]{:S(2)}) copy-start(bf16[360,768]{1,0:T(8,128)(2,1)} %reshape.373) | copy-start | bytes 1658884
  104.5 15.7 %all-to-all-start.4 = ((f32[2,16,4,768]{3,2,0,1:T(4,128)}), f32[2,16,4,768]{3,2,0,1:T(4,128)S(1)}, u32[]{:S(2)}, u32[]{:S(2)}) async-start(f32[2,16,4,768]{3,2,0,1:T(4,128)} %copy.155), calls=%async_computation.4 | async-start | bytes 786432 | tf_op jit(solution)/shard_map/all_to_all | solution.py:126
  108.1 142.2 %reduce-scatter.9.cloned.1.call-start = ((), (), s32[]{:S(2)}) async-start(), calls=%async_computation.13 | async-start | bytes 14155776 | tf_op jit(solution)/shard_map/reduce_scatter | solution.py:186
  139.4 225.4 %reduce-scatter.11.cloned.1.call-start = ((), (), s32[]{:S(2)}) async-start(), calls=%async_computation.14 | async-start | bytes 14155776 | tf_op jit(solution)/shard_map/reduce_scatter | solution.py:187
  162.5 15.9 %all-to-all-start.6 = ((f32[2,1,64,768]{3,0,1,2:T(2,128)}), f32[2,1,64,768]{3,0,1,2:T(2,128)S(1)}, u32[]{:S(2)}, u32[]{:S(2)}) async-start(f32[2,1,64,768]{3,0,1,2:T(2,128)} %copy.160), calls=%async_computation.6 | async-start | bytes 786432 | tf_op jit(solution)/shard_map/all_to_all | solution.py:151
  178.4 15.7 %all-to-all-start.5 = ((f32[2,1,64,768]{3,0,1,2:T(2,128)}), f32[2,1,64,768]{3,0,1,2:T(2,128)S(1)}, u32[]{:S(2)}, u32[]{:S(2)}) async-start(f32[2,1,64,768]{3,0,1,2:T(2,128)} %copy.158), calls=%async_computation.5 | async-start | bytes 786432 | tf_op jit(solution)/shard_map/all_to_all | solution.py:152
  181.9 261.8 %all-reduce.16.cloned.1.call-start = ((), (), s32[]{:S(2)}) async-start(), calls=%async_computation.17 | async-start | bytes 3145728 | tf_op jit(solution)/shard_map/psum | solution.py:172
  198.7 3.4 copy-start.8
  203.3 2.3 copy-start.9
  216.7 280.7 %reduce-scatter.13.cloned.1.call-start = ((), (), s32[]{:S(2)}) async-start(), calls=%async_computation.15 | async-start | bytes 5013504
  256.4 275.0 %reduce-scatter.15.cloned.1.call-start = ((), (), s32[]{:S(2)}) async-start(), calls=%async_computation.16 | async-start | bytes 5013504
  378.2 17.9 %all-to-all-start.8 = ((f32[2,16,4,768]{3,2,0,1:T(4,128)}), f32[2,16,4,768]{3,2,0,1:T(4,128)S(1)}, u32[]{:S(2)}, u32[]{:S(2)}) async-start(f32[2,16,4,768]{3,2,0,1:T(4,128)} %copy.176), calls=%async_computation.8 | async-start | bytes 786432 | tf_op jit(solution)/shard_map/all_to_all | solution.py:161
  396.2 50.4 %all-to-all-start.7 = ((f32[2,16,4,768]{3,2,0,1:T(4,128)}), f32[2,16,4,768]{3,2,0,1:T(4,128)S(1)}, u32[]{:S(2)}, u32[]{:S(2)}) async-start(f32[2,16,4,768]{3,2,0,1:T(4,128)} %copy.173), calls=%async_computation.7 | async-start | bytes 786432 | tf_op jit(solution)/shard_map/all_to_all | solution.py:160
  (21 other events, 29.2 us)
Sparse Core Ops, SparseCore 0:
  139.5 110.7 reduce-scatter.8
  252.6 112.1 reduce-scatter.10
  368.6 83.4 reduce-scatter.12
  455.8 75.5 reduce-scatter.14
Sparse Core Ops, SparseCore 1:
  216.7 226.9 all-reduce.15
where the time goes:
time: 549 us; the launch traced here: 541 us
  waiting for transfers between devices  294 us (54%)
  matrix products  88.4 us (16%)
  local copies, waits for them, and re-layouts  44.3 us (8%)
  blocking collectives  41.9 us (8%)
  starting transfers between devices  40.8 us (7%)
  between operations  16.4 us (3%)
  other arithmetic  14.9 us (3%)
    reduce_scatter x1, waiting for transfers between devices, local(): lax.psum_scatter(term_two, 'dp', scatter_dimension=1, tiled=True)  108 us
    psum x1, waiting for transfers between devices, local(): lax.psum((grad_gain_one, grad_gain_two, pulled[2], pulled[3], pulled[4],...  43.3 us
    psum x1, blocking collectives, local(): lax.psum((grad_gain_one, grad_gain_two, pulled[2], pulled[3], pulled[4],...  41.9 us
    reduce_scatter x1, waiting for transfers between devices, local(): lax.psum_scatter(term_one, 'dp', scatter_dimension=1, tiled=True)  33.6 us
    unnamed x7, waiting for transfers between devices  32.1 us
    unnamed x69, local copies, waits for them, and re-layouts  19.4 us
    dot_general x16, matrix products, meridian_apply(): return jnp.einsum('hk,bhmd->bkmd', table, field, precision=highest)  14.6 us
    all_to_all x1, waiting for transfers between devices, local(): lax.all_to_all(stash, 'space', split_axis=1, concat_axis=0, tiled=True)  12.9 us
  transfers between devices with their start and end apart: 14, of which 12 were waited for; matrix products, arithmetic and copies ran while one was open for 18% of the time, Pallas kernels for 0%

commit v1 on v0

--- a/solution.py
+++ b/solution.py
@@ -7,6 +7,7 @@
 KW = 64
 epsilon = 1e-05
 highest = lax.Precision.HIGHEST
+post_the_skins = lambda across, axis_id, x_local: lax.psum(lax.psum(x_local, across), axis_id)
 
 
 def layer_norm(values, gain_vector):
@@ -169,7 +170,9 @@
     grad_input = grad_mixed + grad_base
     bias_sum = jnp.sum(grad_hidden, axis=0)
     out_sum = jnp.sum(cotangent, axis=(0, 1, 2), dtype=jnp.float32)
-    totals = lax.psum(
+    totals = post_the_skins(
+        "dp",
+        "space",
         (
             grad_gain_one,
             grad_gain_two,
@@ -180,7 +183,6 @@
             bias_sum,
             out_sum,
         ),
-        ("dp", "space"),
     )
     paired = (
         lax.psum_scatter(term_one, "dp", scatter_dimension=1, tiled=True),

time: 549 us -> 759 us (1.38)
  waiting for transfers between devices: 294 us -> 473 us
  blocking collectives: 41.9 us -> 66.1 us
    unnamed x7 -> x8, waiting for transfers between devices: 32.1 us -> 128 us
    reduce_scatter x1, waiting for transfers between devices: 33.6 us -> 113 us  [local(): lax.psum_scatter(term_one, 'dp', scatter_dimension=1, tiled=True)]
    psum x1 -> x2, blocking collectives: 41.9 us -> 66.1 us  [the longest x1 59.1 us: lax.psum(lax.psum(x_local, across), axis_id)]
    all_to_all x1, waiting for transfers between devices: 0.01 us -> 13.1 us  [local(): lax.all_to_all(grad_merid_real, 'space', split_axis=1, concat_axis=2, til...]
    psum x1 -> x2, waiting for transfers between devices: 43.3 us -> 32.7 us  [the longest x1 32.7 us: lax.psum(x_local, across)]
    unnamed x69 -> x85, local copies, waits for them, and re-layouts: 19.4 us -> 21 us
  transfers between devices with their start and end apart: 14 -> 15, of which waited for: 12 -> 14; matrix products, arithmetic and copies ran while one was open for 18% -> 10% of each run, Pallas kernels for 0% -> 0%
where the time goes in v1:
time: 759 us; the launch traced here: 751 us
  waiting for transfers between devices  473 us (62%)
  matrix products  93.1 us (12%)
  blocking collectives  66.1 us (9%)
  local copies, waits for them, and re-layouts  45.9 us (6%)
  starting transfers between devices  41.7 us (5%)
  other arithmetic  16 us (2%)
  between operations  15.6 us (2%)
    unnamed x8, waiting for transfers between devices  128 us
    reduce_scatter x1, waiting for transfers between devices, local(): lax.psum_scatter(term_one, 'dp', scatter_dimension=1, tiled=True)  113 us
    reduce_scatter x1, waiting for transfers between devices, local(): lax.psum_scatter(term_two, 'dp', scatter_dimension=1, tiled=True)  107 us
    psum x1, blocking collectives, lax.psum(lax.psum(x_local, across), axis_id)  59.1 us
    psum x1, waiting for transfers between devices, lax.psum(x_local, across)  32.7 us
    unnamed x85, local copies, waits for them, and re-layouts  21 us
    dot_general x16, matrix products, meridian_apply(): return jnp.einsum('hk,bhmd->bkmd', table, field, precision=highest)  15.4 us
  transfers between devices with their start and end apart: 15, of which 14 were waited for; matrix products, arithmetic and copies ran while one was open for 10% of the time, Pallas kernels for 0%

profile of v1, /device:TPU:0, one launch (start us, length us, event | category | flops | bytes accessed | tf_op | source)
XLA Modules:
  0.0 751.2 jit_solution(2264385408436756193)
XLA Ops:
  7.2 7.4 all-to-all-start
  16.5 12.9 %all-to-all-done = bf16[1,16,2,8640]{3,2,0,1:T(2,128)(2,1)S(1)} async-done(((bf16[1,16,2,8640]{3,2,0,1:T(2,128)(2,1)}), bf16[1,16,2,8640]{3,2,0,1:T(2,128)(2,1)S(1)}, u32[]{:S(2)}, u32[]{:S(2)}) %all-to-all-start) | async-done | bytes 552992 | tf_op jit(solution)/shard_map/all_to_all | solution.py:103
  43.1 9.8 %all-to-all-done.1 = f32[2,1,64,768]{3,0,1,2:T(2,128)S(1)} async-done(((f32[2,1,64,768]{3,0,1,2:T(2,128)}), f32[2,1,64,768]{3,0,1,2:T(2,128)S(1)}, u32[]{:S(2)}, u32[]{:S(2)}) %all-to-all-start.1) | async-done | bytes 393248 | tf_op jit(solution)/shard_map/all_to_all | solution.py:117
  58.4 10.4 %all-to-all-done.2 = f32[2,1,64,768]{3,0,1,2:T(2,128)S(1)} async-done(((f32[2,1,64,768]{3,0,1,2:T(2,128)}), f32[2,1,64,768]{3,0,1,2:T(2,128)S(1)}, u32[]{:S(2)}, u32[]{:S(2)}) %all-to-all-start.2) | async-done | bytes 393248 | tf_op jit(solution)/shard_map/all_to_all | solution.py:118
  94.2 9.1 %all-to-all-done.3 = f32[2,16,4,768]{3,2,0,1:T(4,128)S(1)} async-done(((f32[2,16,4,768]{3,2,0,1:T(4,128)}), f32[2,16,4,768]{3,2,0,1:T(4,128)S(1)}, u32[]{:S(2)}, u32[]{:S(2)}) %all-to-all-start.3) | async-done | bytes 393248 | tf_op jit(solution)/shard_map/all_to_all | solution.py:126
  107.3 6.4 fusion.368
  122.7 9.5 %fusion.363 = (f32[3072]{0:T(1024)S(1)}, bf16[360,3072]{1,0:T(8,128)(2,1)S(1)}, f32[360,3072]{1,0:T(8,128)}) fusion(f32[360,3072]{1,0:T(8,128)} %fusion.368, f32[3072]{0:T(1024)S(1)} %copy-done.38, bf16[360,768]{1,0:T(8,128)(2,1)S(1)} %reshape.380, bf16[768,3072]{1,0:T(8,128)(2,1)} %param.20), kind=kOutput, calls=%fused_computation.455 | convolution fusion | flops 1723020288 | bytes 16355328 | tf_op jit(solution)/shard_map/dot_general | solution.py:133
  133.5 5.2 fusion.34
  151.8 10.0 %all-to-all-done.5 = f32[2,1,64,768]{3,0,1,2:T(2,128)S(1)} async-done(((f32[2,1,64,768]{3,0,1,2:T(2,128)}), f32[2,1,64,768]{3,0,1,2:T(2,128)S(1)}, u32[]{:S(2)}, u32[]{:S(2)}) %all-to-all-start.5) | async-done | bytes 393248 | tf_op jit(solution)/shard_map/all_to_all | solution.py:153
  166.9 10.6 %all-to-all-done.6 = f32[2,1,64,768]{3,0,1,2:T(2,128)S(1)} async-done(((f32[2,1,64,768]{3,0,1,2:T(2,128)}), f32[2,1,64,768]{3,0,1,2:T(2,128)S(1)}, u32[]{:S(2)}, u32[]{:S(2)}) %all-to-all-start.6) | async-done | bytes 393248 | tf_op jit(solution)/shard_map/all_to_all | solution.py:152
  204.8 6.7 fusion.32
  212.6 8.9 %convolution_bitcast_fusion = f32[768,3072]{0,1:T(8,128)} fusion(bf16[360,768]{1,0:T(8,128)(2,1)S(1)} %copy-done.32, f32[360,3072]{1,0:T(8,128)} %get-tuple-element.91), kind=kOutput, calls=%fused_computation.3 | convolution fusion | flops 1708646400 | bytes 14413824 | tf_op jit(solution)/shard_map/td,tf->df/dot_general | solution.py:146
  221.5 32.7 %all-reduce.21.cloned.1.call-done = (f32[2,8,96,96]{3,2,1,0:T(8,128)}, f32[2,8,96,96]{3,2,1,0:T(8,128)}) async-done(((f32[2,8,96,96]{3,2,1,0:T(8,128)}, f32[2,8,96,96]{3,2,1,0:T(8,128)}), (f32[2,8,96,96]{3,2,1,0:T(8,128)}, f32[2,8,96,96]{3,2,1,0:T(8,128)})) %all-reduce.21.cloned.1.call-update) | async-done | bytes 1179664 | tf_op jit(solution)/shard_map/psum | solution.py:10
  254.3 112.9 %reduce-scatter.9.cloned.1.call-done = f32[768,1536]{1,0:T(8,128)} async-done(((f32[768,3072]{1,0:T(8,128)}), f32[768,1536]{1,0:T(8,128)}) %reduce-scatter.9.cloned.1.call-update) | async-done | bytes 4718608 | tf_op jit(solution)/shard_map/reduce_scatter | solution.py:188
  367.2 6.1 copy.208
  373.6 106.6 %reduce-scatter.11.cloned.1.call-done = f32[768,1536]{0,1:T(8,128)} async-done(((f32[768,3072]{0,1:T(8,128)}), f32[768,1536]{0,1:T(8,128)}) %reduce-scatter.11.cloned.1.call-update) | async-done | bytes 4718608 | tf_op jit(solution)/shard_map/reduce_scatter | solution.py:189
  493.6 5.6 all-to-all-start.8
  501.3 12.9 %all-to-all-done.8 = f32[2,16,4,768]{3,2,0,1:T(4,128)S(1)} async-done(((f32[2,16,4,768]{3,2,0,1:T(4,128)}), f32[2,16,4,768]{3,2,0,1:T(4,128)S(1)}, u32[]{:S(2)}, u32[]{:S(2)}) %all-to-all-start.8) | async-done | bytes 393248 | tf_op jit(solution)/shard_map/all_to_all | solution.py:162
  514.2 5.2 all-to-all-start.7
  519.8 13.1 %all-to-all-done.7 = f32[2,16,4,768]{3,2,0,1:T(4,128)S(1)} async-done(((f32[2,16,4,768]{3,2,0,1:T(4,128)}), f32[2,16,4,768]{3,2,0,1:T(4,128)S(1)}, u32[]{:S(2)}, u32[]{:S(2)}) %all-to-all-start.7) | async-done | bytes 393248 | tf_op jit(solution)/shard_map/all_to_all | solution.py:161
  539.3 7.0 all-reduce.14
  546.3 59.1 %all-reduce.12 = (f32[3072]{0:T(1024)S(1)}, f32[768]{0:T(1024)S(1)}, f32[768]{0:T(1024)S(1)}, f32[768]{0:T(1024)S(1)}, f32[2,768]{1,0:T(2,128)S(1)}, /*index=5*/f32[2,768]{1,0:T(2,128)S(1)}) all-reduce(f32[3072]{0:T(1024)S(1)} %get-tuple-element.73, f32[768]{0:T(1024)S(1)} %get-tuple-element.74, ...), channel_id=1, replica_groups=mesh['dp'=2,'space'=16] {'space'}, use_global_device_ids=true, to_apply=%region_15.16 | all-reduce | flops 8448 | bytes 67584 | tf_op jit(solution)/shard_map/psum | solution.py:10
  612.1 51.2 %reduce-scatter.13.cloned.1.call-done = f32[96,768]{1,0:T(8,128)} async-done(((f32[1536,768]{1,0:T(8,128)}), f32[96,768]{1,0:T(8,128)}) %reduce-scatter.13.cloned.1.call-update) | async-done | bytes 294928
  665.3 76.5 %reduce-scatter.15.cloned.1.call-done = f32[96,768]{1,0:T(8,128)} async-done(((f32[1536,768]{1,0:T(8,128)}), f32[96,768]{1,0:T(8,128)}) %reduce-scatter.15.cloned.1.call-update) | async-done | bytes 294928
  (231 shorter events, 140.0 us)
Async XLA Ops:
  7.2 22.2 %all-to-all-start = ((bf16[1,16,2,8640]{3,2,0,1:T(2,128)(2,1)}), bf16[1,16,2,8640]{3,2,0,1:T(2,128)(2,1)S(1)}, u32[]{:S(2)}, u32[]{:S(2)}) async-start(bf16[1,16,2,8640]{3,2,0,1:T(2,128)(2,1)} %bitcast.441), calls=%async_computation | async-start | bytes 1114112 | tf_op jit(solution)/shard_map/all_to_all | solution.py:103
  36.4 16.5 %all-to-all-start.1 = ((f32[2,1,64,768]{3,0,1,2:T(2,128)}), f32[2,1,64,768]{3,0,1,2:T(2,128)S(1)}, u32[]{:S(2)}, u32[]{:S(2)}) async-start(f32[2,1,64,768]{3,0,1,2:T(2,128)} %copy.140), calls=%async_computation.1 | async-start | bytes 786432 | tf_op jit(solution)/shard_map/all_to_all | solution.py:117
  42.0 14.7 %copy-start.36 = (f32[2,768]{1,0:T(2,128)S(1)}, f32[2,768]{1,0:T(2,128)}, u32[]{:S(2)}) copy-start(f32[2,768]{1,0:T(2,128)} %param.16) | copy-start | bytes 18436
  42.0 14.9 %copy-start.37 = (f32[2,768]{1,0:T(2,128)S(1)}, f32[2,768]{1,0:T(2,128)}, u32[]{:S(2)}) copy-start(f32[2,768]{1,0:T(2,128)} %param.18) | copy-start | bytes 18436
  52.9 15.9 %all-to-all-start.2 = ((f32[2,1,64,768]{3,0,1,2:T(2,128)}), f32[2,1,64,768]{3,0,1,2:T(2,128)S(1)}, u32[]{:S(2)}, u32[]{:S(2)}) async-start(f32[2,1,64,768]{3,0,1,2:T(2,128)} %copy.142), calls=%async_computation.2 | async-start | bytes 786432 | tf_op jit(solution)/shard_map/all_to_all | solution.py:118
  86.1 5.1 copy-start.21
  87.6 15.7 %all-to-all-start.3 = ((f32[2,16,4,768]{3,2,0,1:T(4,128)}), f32[2,16,4,768]{3,2,0,1:T(4,128)S(1)}, u32[]{:S(2)}, u32[]{:S(2)}) async-start(f32[2,16,4,768]{3,2,0,1:T(4,128)} %copy.152), calls=%async_computation.3 | async-start | bytes 786432 | tf_op jit(solution)/shard_map/all_to_all | solution.py:126
  93.2 14.1 %copy-start.31 = (bf16[360,768]{1,0:T(8,128)(2,1)S(1)}, bf16[360,768]{1,0:T(8,128)(2,1)}, u32[]{:S(2)}) copy-start(bf16[360,768]{1,0:T(8,128)(2,1)} %reshape.373) | copy-start | bytes 1658884
  103.3 16.1 %all-to-all-start.4 = ((f32[2,16,4,768]{3,2,0,1:T(4,128)}), f32[2,16,4,768]{3,2,0,1:T(4,128)S(1)}, u32[]{:S(2)}, u32[]{:S(2)}) async-start(f32[2,16,4,768]{3,2,0,1:T(4,128)} %copy.155), calls=%async_computation.4 | async-start | bytes 786432 | tf_op jit(solution)/shard_map/all_to_all | solution.py:127
  122.7 9.5 %copy-start.23 = (bf16[360,768]{1,0:T(8,128)(2,1)}, bf16[360,768]{1,0:T(8,128)(2,1)S(1)}, u32[]{:S(2)}) copy-start(bf16[360,768]{1,0:T(8,128)(2,1)S(1)} %reshape.380) | copy-start | bytes 1658884
  146.1 15.7 %all-to-all-start.5 = ((f32[2,1,64,768]{3,0,1,2:T(2,128)}), f32[2,1,64,768]{3,0,1,2:T(2,128)S(1)}, u32[]{:S(2)}, u32[]{:S(2)}) async-start(f32[2,1,64,768]{3,0,1,2:T(2,128)} %copy.158), calls=%async_computation.5 | async-start | bytes 786432 | tf_op jit(solution)/shard_map/all_to_all | solution.py:153
  161.8 17.0 %copy-start.14 = (f32[2,1,64,768]{3,0,1,2:T(2,128)}, f32[2,1,64,768]{3,0,1,2:T(2,128)S(1)}, u32[]{:S(2)}) copy-start(f32[2,1,64,768]{3,0,1,2:T(2,128)S(1)} %all-to-all-done.5) | copy-start | bytes 1179652
  161.8 15.7 %all-to-all-start.6 = ((f32[2,1,64,768]{3,0,1,2:T(2,128)}), f32[2,1,64,768]{3,0,1,2:T(2,128)S(1)}, u32[]{:S(2)}, u32[]{:S(2)}) async-start(f32[2,1,64,768]{3,0,1,2:T(2,128)} %copy.160), calls=%async_computation.6 | async-start | bytes 786432 | tf_op jit(solution)/shard_map/all_to_all | solution.py:152
  165.3 88.9 %all-reduce.21.cloned.1.call-start = ((), (), s32[]{:S(2)}) async-start(), calls=%async_computation.18 | async-start | bytes 3145728 | tf_op jit(solution)/shard_map/psum | solution.py:10
  180.7 4.5 copy-start.15
  180.7 4.5 copy-start.28
  191.1 4.4 copy-start.9
  203.8 163.4 %reduce-scatter.9.cloned.1.call-start = ((), (), s32[]{:S(2)}) async-start(), calls=%async_computation.13 | async-start | bytes 14155776 | tf_op jit(solution)/shard_map/reduce_scatter | solution.py:188
  211.5 268.6 %reduce-scatter.11.cloned.1.call-start = ((), (), s32[]{:S(2)}) async-start(), calls=%async_computation.14 | async-start | bytes 14155776 | tf_op jit(solution)/shard_map/reduce_scatter | solution.py:189
  221.5 387.5 %all-reduce.19.cloned.1.call-start = ((), (), s32[]{:S(2)}) async-start(), calls=%async_computation.17 | async-start | bytes 3145728 | tf_op jit(solution)/shard_map/psum | solution.py:10
  254.3 409.0 %reduce-scatter.13.cloned.1.call-start = ((), (), s32[]{:S(2)}) async-start(), calls=%async_computation.15 | async-start | bytes 5013504
  373.3 368.5 %reduce-scatter.15.cloned.1.call-start = ((), (), s32[]{:S(2)}) async-start(), calls=%async_computation.16 | async-start | bytes 5013504
  493.6 20.6 %all-to-all-start.8 = ((f32[2,16,4,768]{3,2,0,1:T(4,128)}), f32[2,16,4,768]{3,2,0,1:T(4,128)S(1)}, u32[]{:S(2)}, u32[]{:S(2)}) async-start(f32[2,16,4,768]{3,2,0,1:T(4,128)} %copy.176), calls=%async_computation.8 | async-start | bytes 786432 | tf_op jit(solution)/shard_map/all_to_all | solution.py:162
  514.2 18.7 %all-to-all-start.7 = ((f32[2,16,4,768]{3,2,0,1:T(4,128)}), f32[2,16,4,768]{3,2,0,1:T(4,128)S(1)}, u32[]{:S(2)}, u32[]{:S(2)}) async-start(f32[2,16,4,768]{3,2,0,1:T(4,128)} %copy.173), calls=%async_computation.7 | async-start | bytes 786432 | tf_op jit(solution)/shard_map/all_to_all | solution.py:161
  (30 other events, 52.4 us)
Sparse Core Ops, SparseCore 0:
  203.9 50.2 all-reduce.20
  256.5 110.6 reduce-scatter.8
  369.5 110.6 reduce-scatter.10
  483.6 101.3 all-reduce.18
  588.7 74.5 reduce-scatter.12
  667.0 74.7 reduce-scatter.14
